TPU v7x, 256 devices: a whole 4x4x8 slice. The times are simulated.
256 devices in a mesh: dp: 32 (over x, z_hi, core), space: 8 (over y, z_lo).
Axes of the slice: x: 4, y: 4, z: 8 (z_hi: 4, z_lo: 2; z = z_hi * 2 + z_lo), core: 2. Of those that a mesh axis runs over, the one named last changes fastest.
Arguments:
- layer_input: bfloat16 [32, 32, 16, 16, 128], P('dp', None, 'space'), may hold values from -6 to 6
- pre_act: bfloat16 [32, 32, 16, 16, 128], P('dp', None, 'space'), may hold values from -6 to 6
- cotangent: bfloat16 [32, 32, 16, 16, 128], P('dp', None, 'space'), may hold values from -6 to 6
- weight_one: bfloat16 [3, 3, 3, 32, 32], replicated, may hold values from -0.21875 to 0.21875
- weight_two: bfloat16 [3, 3, 3, 32, 32], replicated, may hold values from -0.21875 to 0.21875
Outputs:
- grad_input: bfloat16 [32, 32, 16, 16, 128], P('dp', None, 'space')
- grad_one: float32 [3, 3, 3, 32, 32], replicated
- grad_two: float32 [3, 3, 3, 32, 32], replicated
All inputs are finite; a program needn't handle non-finite values.
Results may differ from a plain program's by a relative error of at most 0.0049.
Values may be sent and summed in bfloat16 or wider, within the bound.
A program may use at most 64 MiB of HBM per device.

v0:
```python
import jax
import jax.numpy as jnp
from jax import lax
from jax.sharding import PartitionSpec as P


def padded(block, sides, width):
    for axis, dim in sides:
        count = lax.axis_size(axis)
        forward = [(i, i + 1) for i in range(count - 1)]
        backward = [(target, source) for source, target in forward]
        low = lax.ppermute(
            lax.slice_in_dim(block, block.shape[dim] - width, None, axis=dim), axis, forward
        )
        high = lax.ppermute(lax.slice_in_dim(block, 0, width, axis=dim), axis, backward)
        block = jnp.concatenate([low, block, high], axis=dim)
    return block


def leaky(value):
    return jnp.where(value > 0, value, 0.3 * value)


def pad_plane(value):
    widths = [(0, 0)] * (value.ndim - 2) + [(1, 1), (1, 1)]
    return jnp.pad(value, widths)


def kernel_grad(top, low_pad):
    depth, height, width = (top.shape[1], top.shape[2], top.shape[3])
    rows = []
    for kd in range(3):
        for kh in range(3):
            for kw in range(3):
                window = low_pad[:, kd : kd + depth, kh : kh + height, kw : kw + width]
                rows.append(
                    jnp.einsum("odhw,idhw->oi", top, window, preferred_element_type=jnp.float32)
                )
    return jnp.stack(rows).reshape(3, 3, 3, top.shape[0], low_pad.shape[0])


def transposed(top_pad, weight, depth):
    height, width = (top_pad.shape[2] - 2, top_pad.shape[3] - 2)
    total = jnp.zeros((weight.shape[4], depth, height, width), jnp.float32)
    for kd in range(3):
        for kh in range(3):
            for kw in range(3):
                window = top_pad[
                    :, 2 - kd : 2 - kd + depth, 2 - kh : 2 - kh + height, 2 - kw : 2 - kw + width
                ]
                total = total + jnp.einsum(
                    "oi,odhw->idhw", weight[kd, kh, kw], window, preferred_element_type=jnp.float32
                )
    return total


def per_device(layer_input, pre_act, cotangent, weight_one, weight_two):
    source, pre, cot = (layer_input[0], pre_act[0], cotangent[0])
    depth, height, width = (source.shape[1], source.shape[2], source.shape[3])
    stacked = jnp.stack([source, pre, cot])
    extended = padded(stacked, (("space", 2),), 1)
    source_ext, pre_ext, cot_ext = (extended[0], extended[1], extended[2])
    activation = leaky(pre_ext.astype(jnp.float32)).astype(jnp.bfloat16)
    gtwo = kernel_grad(cot, pad_plane(activation))
    grad_act = transposed(pad_plane(cot_ext), weight_two, depth)
    grad_pre = (grad_act * jnp.where(pre > 0, 1.0, 0.3)).astype(jnp.bfloat16)
    grad_ext = padded(grad_pre, (("space", 1),), 1)
    scale = (lax.axis_size("dp") * lax.axis_size("space") * depth * height * width) ** (-0.5)
    gtwo = lax.psum(gtwo, ("dp", "space"))
    gone = kernel_grad(grad_pre, pad_plane(source_ext))
    gone = lax.psum(gone, ("dp", "space"))
    grad_in = transposed(pad_plane(grad_ext), weight_one, depth).astype(jnp.bfloat16)
    return (grad_in[None], gone * scale, gtwo * scale)


def solution(mesh):
    in_specs = (
        P("dp", None, "space", None, None),
        P("dp", None, "space", None, None),
        P("dp", None, "space", None, None),
        P(),
        P(),
    )
    out_specs = (P("dp", None, "space", None, None), P(), P())
    return jax.shard_map(
        per_device, mesh=mesh, in_specs=in_specs, out_specs=out_specs, check_vma=False
    )
```

profile of v0, /device:TPU:1, one launch (start us, length us, event | category | flops | bytes accessed | tf_op | source)
XLA Modules:
  0.0 335.7 jit_solution(16639018770619011474)
XLA Ops:
  7.2 1.1 copy_dynamic-update-slice_fusion.1
  8.3 1.1 copy_dynamic-update-slice_fusion.2
  9.6 4.4 %collective-permute-start = (bf16[3,32,1,16,128]{4,1,3,2,0:T(8,128)(2,1)S(1)}, bf16[3,32,1,16,128]{4,1,3,2,0:T(8,128)(2,1)S(1)}, u32[]{:S(2)}, u32[]{:S(2)}) collective-permute-start(bf16[3,32,1,16,128]{4,1,3,2,0:T(8,128)(2,1)S(1)} %get-tuple-element.10), channel_id=1, source_target_pairs={{0,1},{1,2},{2,3},{3,4},{4,5},{5,6},{6,7},{8,9},{9,10},{10,11},{11... | collective-permute-start | bytes 1179656 | tf_op jit(solution)/shard_map/ppermute | solution.py:12
  14.0 1.3 collective-permute-start.1
  15.3 6.5 %collective-permute-done = bf16[3,32,1,16,128]{4,1,3,2,0:T(8,128)(2,1)S(1)} collective-permute-done((bf16[3,32,1,16,128]{4,1,3,2,0:T(8,128)(2,1)S(1)}, bf16[3,32,1,16,128]{4,1,3,2,0:T(8,128)(2,1)S(1)}, u32[]{:S(2)}, u32[]{:S(2)}) %collective-permute-start) | collective-permute-done | bytes 393248 | tf_op jit(solution)/shard_map/ppermute | solution.py:12
  21.8 10.0 %collective-permute-done.1 = bf16[3,32,1,16,128]{4,1,3,2,0:T(8,128)(2,1)S(1)} collective-permute-done((bf16[3,32,1,16,128]{4,1,3,2,0:T(8,128)(2,1)S(1)}, bf16[3,32,1,16,128]{4,1,3,2,0:T(8,128)(2,1)S(1)}, u32[]{:S(2)}, u32[]{:S(2)}) %collective-permute-start.1) | collective-permute-done | bytes 393248 | tf_op jit(solution)/shard_map/ppermute | solution.py:15
  33.0 0.3 fusion.56
  35.4 0.3 fusion.48
  37.8 0.3 fusion.40
  39.5 1.0 copy.93
  40.7 0.3 convolution_add_fusion.30
  41.0 0.3 convolution_add_fusion.29
  41.3 0.3 convolution_add_fusion.28
  41.8 0.3 convolution_add_fusion.26
  42.1 0.3 convolution_add_fusion.25
  42.7 0.3 convolution_add_fusion.23
  43.0 0.3 convolution_add_fusion.22
  43.5 0.3 convolution_add_fusion.20
  43.8 0.3 convolution_add_fusion.19
  44.4 0.3 convolution_add_fusion.17
  44.7 0.3 convolution_add_fusion.16
  45.2 0.3 fusion.22
  45.5 0.3 fusion.21
  46.1 0.3 fusion.19
  46.4 0.3 fusion.18
  46.9 0.3 fusion.16
  47.2 0.3 fusion.15
  47.8 0.7 copy-done.1
  48.5 0.3 fusion.27
  49.3 0.3 fusion.84
  49.6 0.3 fusion.83
  50.1 0.3 fusion.81
  51.6 0.3 fusion.75
  51.9 0.3 fusion.74
  52.4 0.3 fusion.72
  53.2 0.3 fusion.69
  53.5 0.3 fusion.68
  54.0 0.3 fusion.66
  54.3 0.3 fusion.65
  54.8 0.3 fusion.63
  55.1 0.3 fusion.62
  55.9 0.8 copy-done.2
  56.8 3.5 %collective-permute-start.2 = (bf16[32,1,16,128]{3,0,2,1:T(8,128)(2,1)S(1)}, bf16[32,1,16,128]{3,0,2,1:T(8,128)(2,1)S(1)}, u32[]{:S(2)}, u32[]{:S(2)}) collective-permute-start(bf16[32,1,16,128]{3,0,2,1:T(8,128)(2,1)S(1)} %get-tuple-element.12), channel_id=1, source_target_pairs={{0,1},{1,2},{2,3},{3,4},{4,5},{5,6},{6,7},{8,9},{9,10},{10,11},{11... | collective-permute-start | bytes 393224 | tf_op jit(solution)/shard_map/ppermute | solution.py:12
  60.3 1.3 collective-permute-start.3
  61.6 255.8 %all-reduce.7.cloned.1.call-done = (f32[3,3,3,32,32]{4,3,2,1,0:T(8,128)}, f32[3,3,3,32,32]{4,3,2,1,0:T(8,128)}) async-done(((f32[3,3,3,32,32]{4,3,2,1,0:T(8,128)}, f32[3,3,3,32,32]{4,3,2,1,0:T(8,128)}), (f32[3,3,3,32,32]{4,3,2,1,0:T(8,128)}, f32[3,3,3,32,32]{4,3,2,1,0:T(8,128)})) %all-reduce.7.cloned.1.call-update) | async-done | bytes 221200 | tf_op jit(solution)/shard_map/psum | solution.py:71
  317.4 2.1 broadcast_multiply_fusion
  319.5 0.5 select_maximum_fusion
  320.1 0.4 copy-done.4
  320.5 0.3 fusion.118
  321.3 0.3 convolution_add_fusion.14
  321.8 0.3 convolution_add_fusion.12
  322.4 0.3 convolution_add_fusion.10
  322.7 0.3 convolution_add_fusion.9
  323.2 0.3 convolution_add_fusion.7
  323.5 0.3 convolution_add_fusion.6
  324.1 0.3 convolution_add_fusion.4
  324.9 0.3 convolution_add_fusion.1
  325.2 0.3 fusion.12
  325.8 0.3 fusion.10
  326.1 0.3 fusion.9
  326.6 0.3 fusion.7
  327.2 0.3 fusion.5
  327.5 0.3 fusion.4
  328.1 0.8 copy.94
  (77 shorter events, 16.0 us)
Async XLA Ops:
  7.2 2.2 copy-start
  7.2 310.2 %all-reduce.7.cloned.1.call-start = ((), (), s32[]{:S(2)}) async-start(), calls=%async_computation | async-start | bytes 1769472 | tf_op jit(solution)/shard_map/psum | solution.py:71
  9.6 12.1 %collective-permute-start = (bf16[3,32,1,16,128]{4,1,3,2,0:T(8,128)(2,1)S(1)}, bf16[3,32,1,16,128]{4,1,3,2,0:T(8,128)(2,1)S(1)}, u32[]{:S(2)}, u32[]{:S(2)}) collective-permute-start(bf16[3,32,1,16,128]{4,1,3,2,0:T(8,128)(2,1)S(1)} %get-tuple-element.10), channel_id=1, source_target_pairs={{0,1},{1,2},{2,3},{3,4},{4,5},{5,6},{6,7},{8,9},{9,10},{10,11},{11... | collective-permute-start | bytes 1179656 | tf_op jit(solution)/shard_map/ppermute | solution.py:12
  14.0 17.8 %collective-permute-start.1 = (bf16[3,32,1,16,128]{4,1,3,2,0:T(8,128)(2,1)S(1)}, bf16[3,32,1,16,128]{4,1,3,2,0:T(8,128)(2,1)S(1)}, u32[]{:S(2)}, u32[]{:S(2)}) collective-permute-start(bf16[3,32,1,16,128]{4,1,3,2,0:T(8,128)(2,1)S(1)} %get-tuple-element.11), channel_id=1, source_target_pairs={{1,0},{2,1},{3,2},{4,3},{5,4},{6,5},{7,6},{9,8},{10,9},{11,10},{12... | collective-permute-start | bytes 1179656 | tf_op jit(solution)/shard_map/ppermute | solution.py:15
  39.0 1.5 copy-start.3
  47.5 1.0 copy-start.1
  55.9 0.8 copy-start.2
  56.8 262.8 %collective-permute-start.2 = (bf16[32,1,16,128]{3,0,2,1:T(8,128)(2,1)S(1)}, bf16[32,1,16,128]{3,0,2,1:T(8,128)(2,1)S(1)}, u32[]{:S(2)}, u32[]{:S(2)}) collective-permute-start(bf16[32,1,16,128]{3,0,2,1:T(8,128)(2,1)S(1)} %get-tuple-element.12), channel_id=1, source_target_pairs={{0,1},{1,2},{2,3},{3,4},{4,5},{5,6},{6,7},{8,9},{9,10},{10,11},{11... | collective-permute-start | bytes 393224 | tf_op jit(solution)/shard_map/ppermute | solution.py:12
  60.3 259.2 %collective-permute-start.3 = (bf16[32,1,16,128]{3,0,2,1:T(8,128)(2,1)S(1)}, bf16[32,1,16,128]{3,0,2,1:T(8,128)(2,1)S(1)}, u32[]{:S(2)}, u32[]{:S(2)}) collective-permute-start(bf16[32,1,16,128]{3,0,2,1:T(8,128)(2,1)S(1)} %get-tuple-element.13), channel_id=1, source_target_pairs={{1,0},{2,1},{3,2},{4,3},{5,4},{6,5},{7,6},{9,8},{10,9},{11,10},{12... | collective-permute-start | bytes 393224 | tf_op jit(solution)/shard_map/ppermute | solution.py:15
  319.5 0.9 copy-start.4
Sparse Core Ops, SparseCore 0:
  56.8 260.4 all-reduce.6
where the time goes:
time: 336 us
  waiting for transfers between devices  272 us (81%)
  matrix products  29.2 us (9%)
  between operations  14.5 us (4%)
  starting transfers between devices  10.6 us (3%)
  local copies, waits for them, and re-layouts  6.11 us (2%)
    psum x1, waiting for transfers between devices, per_device(): gone = lax.psum(gone, ('dp', 'space'))  256 us
    dot_general x54, matrix products, transposed(): jnp.einsum('oi,odhw->idhw', weight[kd, kh, kw], window, preferred_element...  15 us
    dot_general x54, matrix products, kernel_grad(): jnp.einsum('odhw,idhw->oi', top, window, preferred_element_type=jnp.float32)  14.3 us
    ppermute x2, waiting for transfers between devices, padded(): lax.ppermute(lax.slice_in_dim(block, 0, width, axis=dim), axis, backward)  10 us
    ppermute x2, starting transfers between devices, padded(): lax.ppermute(lax.slice_in_dim(block, block.shape[dim] - width, None, axis...  7.93 us
  transfers between devices with their start and end apart: 5, of which 3 were waited for; matrix products, arithmetic and copies ran while one was open for 1% of the time, Pallas kernels for 0%

commit v1 on v0

v1 whole, which is shorter than its diff:
```python
import functools

import jax
import jax.numpy as jnp
from jax import lax
from jax.experimental import pallas as pl
from jax.experimental.pallas import tpu as pltpu
from jax.sharding import PartitionSpec as P

CH = 32
HGT = 16
WID = 128
PLANE = HGT * WID
TILES = 32
USED = 27
F32 = jnp.float32
BF16 = jnp.bfloat16


def leaky(value):
    return jnp.where(value > 0, value, 0.3 * value)


def kernel(
    cfg,
    src_hbm, pre_hbm, cot_hbm, w1_ref, w2_ref,
    gin_hbm, g1_ref, g2_ref,
    own, halo, rows_scr, cot3, act3, src3, gp3, preT, wcat, gp_halo, gin_f, gin_v,
    parts, rx0, rx1, rx2, rx3,
    load_sem, out_sem, hs, hr, gs, gr, send_sem, recv_sem,
):
    nx, nzh, ny, nzl, scale = cfg
    nq = nx * ny
    nz = nzh * nzl
    per = TILES // (2 * nq)
    half = TILES // 2
    nsp = ny * nzl
    dp = lax.axis_index("dp")
    sp = lax.axis_index("space")
    core = lax.rem(dp, 2)
    zh = lax.rem(dp // 2, nzh)
    x = dp // (2 * nzh)
    y = sp // nzl
    zl = lax.rem(sp, nzl)
    q = x * ny + y
    z = zh * nzl + zl
    me = core * nq + q

    def plane_peer(slot):
        c = slot // nq
        r = lax.rem(slot, nq)
        return (((r // ny) * nzh + zh) * 2 + c, lax.rem(r, ny) * nzl + zl)

    def z_peer(other):
        return ((x * nzh + other // nzl) * 2 + core, y * nzl + lax.rem(other, nzl))

    has_prev = sp > 0
    has_next = sp < nsp - 1
    barrier = pltpu.get_barrier_semaphore()

    @pl.when(has_prev)
    def _():
        pl.semaphore_signal(barrier, inc=1, device_id=(dp, sp - 1))

    @pl.when(has_next)
    def _():
        pl.semaphore_signal(barrier, inc=1, device_id=(dp, sp + 1))

    def greet_plane(k, carry):
        pl.semaphore_signal(barrier, inc=1, device_id=plane_peer(lax.rem(me + k, 2 * nq)))
        return carry

    def greet_z(k, carry):
        pl.semaphore_signal(barrier, inc=1, device_id=z_peer(lax.rem(z + k, nz)))
        return carry

    lax.fori_loop(1, 2 * nq, greet_plane, 0)
    lax.fori_loop(1, nz, greet_z, 0)

    args = (cot_hbm, src_hbm, pre_hbm)
    loads = [pltpu.make_async_copy(args[k].at[0], own.at[k], load_sem.at[k]) for k in range(3)]
    for copy in loads:
        copy.start()

    expected = 2 * nq - 1 + nz - 1 + has_prev.astype(jnp.int32) + has_next.astype(jnp.int32)
    pl.semaphore_wait(barrier, expected)

    def halo_copy(k, side):
        return pltpu.make_async_remote_copy(
            src_ref=args[k].at[0, :, side],
            dst_ref=halo.at[k, 1 - side],
            send_sem=hs.at[k, side],
            recv_sem=hr.at[k, 1 - side],
            device_id=(dp, sp - 1 if side == 0 else sp + 1),
        )

    for side, there in ((0, has_prev), (1, has_next)):
        @pl.when(there)
        def _():
            for k in range(3):
                halo_copy(k, side).start()

        @pl.when(jnp.logical_not(there))
        def _():
            halo[:, side] = jnp.zeros((3, CH, HGT, WID), BF16)

    for g, w_ref in ((0, w1_ref), (1, w2_ref)):
        for a in range(3):
            for b in range(3):
                block = w_ref[a, b].reshape(3 * CH, CH).astype(F32)
                wcat[g, b * CH:(b + 1) * CH, (2 - a) * 96:(3 - a) * 96] = block.T.astype(BF16)

    lane = lax.broadcasted_iota(jnp.int32, (CH, WID), 1)

    def shifts(value):
        up = jnp.where(lane < WID - 1, pltpu.roll(value, WID - 1, 1), 0.0)
        down = jnp.where(lane > 0, pltpu.roll(value, 1, 1), 0.0)
        return (up, value, down)

    def put_shifted(ref, p, h, value):
        for c, moved in enumerate(shifts(value)):
            ref[p * 96 + c * CH:p * 96 + (c + 1) * CH, h * WID:(h + 1) * WID] = moved.astype(BF16)

    def put_rows(ref, p, h, value):
        moved = value.astype(BF16)
        for b in range(3):
            to = h - b + 1
            if 0 <= to < HGT:
                ref[p * 96 + b * CH:p * 96 + (b + 1) * CH, to * WID:(to + 1) * WID] = moved

    def clear_edges(ref, p):
        blank = jnp.zeros((CH, WID), BF16)
        ref[p * 96:p * 96 + CH, 0:WID] = blank
        ref[p * 96 + 2 * CH:p * 96 + 3 * CH, (HGT - 1) * WID:HGT * WID] = blank

    def turned(k, p, plane):
        rows_scr[k, p] = plane.astype(F32).reshape(CH * HGT, WID)
        return [rows_scr[k, p, pl.ds(h, CH, stride=HGT), :] for h in range(HGT)]

    def take(k, p, plane):
        for h, value in enumerate(turned(k, p, plane)):
            if k == 0:
                put_shifted(cot3, p, h, value)
            elif k == 1:
                put_rows(src3, p, h, value)
            else:
                put_rows(act3, p, h, leaky(value))
                if 1 <= p <= 2:
                    preT[p - 1, :, h * WID:(h + 1) * WID] = value

    for p in range(4):
        clear_edges(src3, p)
        clear_edges(act3, p)
    for k in range(3):
        loads[k].wait()
        for d in range(2):
            take(k, d + 1, own[k, :, d])

    for k in range(3):
        for side, there in ((0, has_prev), (1, has_next)):
            @pl.when(there)
            def _():
                halo_copy(k, 1 - side).wait_recv()
            take(k, 3 * side, halo[k, side])

    def conv(g, ref, d):
        y3 = jnp.dot(wcat[g], ref[d * 96:(d + 3) * 96, :], preferred_element_type=F32)
        blank = jnp.zeros((CH, WID), F32)
        first = jnp.concatenate([y3[0:CH, WID:], blank], axis=1)
        last = jnp.concatenate([blank, y3[2 * CH:, :PLANE - WID]], axis=1)
        return y3[CH:2 * CH] + first + last

    def kernel_grad(low, top):
        total = None
        for d in range(2):
            term = lax.dot_general(
                low[d * 96:(d + 3) * 96, :],
                top[(d + 1) * 96:(d + 1) * 96 + 128, :],
                (((1,), (1,)), ((), ())),
                preferred_element_type=F32,
            )
            total = term if total is None else total + term
        return total

    lane8 = lax.broadcasted_iota(jnp.int32, (9, 8, 128), 2) // CH

    def pack(g, total):
        rows = total.reshape(9, 4, 8, 128)
        for c in range(3):
            tile = None
            for j in range(4):
                piece = rows[:, j]
                shift = ((j - c) * CH) % 128
                if shift:
                    piece = pltpu.roll(piece, shift, 2)
                tile = piece if tile is None else jnp.where(lane8 == j, piece, tile)
            for ab in range(9):
                parts[g, ab * 3 + c] = tile[ab]
        for t in range(USED, TILES):
            parts[g, t] = jnp.zeros((8, 128), F32)

    def rdma(src, dst, g, phase, device):
        return pltpu.make_async_remote_copy(
            src_ref=src, dst_ref=dst, send_sem=send_sem.at[g, phase], recv_sem=recv_sem.at[g, phase], device_id=device
        )

    def pair(g):
        other = 1 - core
        return rdma(parts.at[g, pl.ds(other * half, half)], rx0.at[g], g, 0, (dp + other - core, sp))

    def phase1(g):
        pair(g).wait_recv()
        rx0[g] = rx0[g] + parts[g, pl.ds(core * half, half)]
        rx1[g, q] = rx0[g, pl.ds(q * per, per)]

        def send(k, carry):
            r = lax.rem(q + k, nq)
            rdma(rx0.at[g, pl.ds(r * per, per)], rx1.at[g, q], g, 1, plane_peer(core * nq + r)).start()
            return carry

        lax.fori_loop(1, nq, send, 0)

    def all_of(ref, g, phase, count):
        return rdma(ref.at[g, pl.ds(0, count)], ref.at[g, pl.ds(0, count)], g, phase, (dp + 1 - 2 * core, sp))

    def phase2(g):
        all_of(rx1, g, 1, nq - 1).wait_recv()
        total = rx1[g, 0]
        for r in range(1, nq):
            total = total + rx1[g, r]
        rx2[g, z] = total

        def send(k, carry):
            rdma(rx2.at[g, z], rx2.at[g, z], g, 2, z_peer(lax.rem(z + k, nz))).start()
            return carry

        lax.fori_loop(1, nz, send, 0)

    def phase3(g):
        all_of(rx2, g, 2, nz - 1).wait_recv()
        total = rx2[g, 0]
        for r in range(1, nz):
            total = total + rx2[g, r]
        total = total * scale
        for t in range(per):
            tile = total[t]
            square = jnp.concatenate(
                [tile] + [pltpu.roll(tile, 128 - CH * j, 1) for j in range(1, 4)] + [jnp.zeros((96, 128), F32)], axis=0
            ).T
            mine = None
            for j in range(4):
                piece = square[8 * j:8 * (j + 1)]
                if j:
                    piece = pltpu.roll(piece, CH * j, 1)
                mine = piece if mine is None else mine + piece
            rx3[g, me, t] = mine

        def send(k, carry):
            rdma(rx3.at[g, me], rx3.at[g, me], g, 3, plane_peer(lax.rem(me + k, 2 * nq))).start()
            return carry

        lax.fori_loop(1, 2 * nq, send, 0)

    def finish(g, out_ref):
        all_of(rx3, g, 3, 2 * nq - 1).wait_recv()
        tiles = rx3[g].reshape(TILES, 8, 128)[:USED]
        for j in range(4):
            piece = tiles if j == 0 else pltpu.roll(tiles, 128 - CH * j, 2)
            out_ref[:, 8 * j:8 * (j + 1), :] = piece[:, :, :CH]

    for d in range(2):
        value = conv(1, cot3, d) * jnp.where(preT[d] > 0, 1.0, 0.3)
        for h in range(HGT):
            put_shifted(gp3, d + 1, h, value[:, h * WID:(h + 1) * WID].astype(BF16).astype(F32))

    def gp_copy(side):
        return pltpu.make_async_remote_copy(
            src_ref=gp3.at[pl.ds((1 + side) * 96 + CH, CH)],
            dst_ref=gp_halo.at[1 - side],
            send_sem=gs.at[side],
            recv_sem=gr.at[1 - side],
            device_id=(dp, sp - 1 if side == 0 else sp + 1),
        )

    for side, there in ((0, has_prev), (1, has_next)):
        @pl.when(there)
        def _():
            gp_copy(side).start()

        @pl.when(jnp.logical_not(there))
        def _():
            gp_halo[side] = jnp.zeros((CH, PLANE), BF16)

    gp3[0:96, :] = jnp.zeros((96, PLANE), BF16)
    gp3[288:384, :] = jnp.zeros((96, PLANE), BF16)
    pack(0, kernel_grad(src3, gp3))
    pair(0).start()
    pack(1, kernel_grad(act3, cot3))
    pair(1).start()
    phase1(0)
    phase1(1)

    for side, there in ((0, has_prev), (1, has_next)):
        @pl.when(there)
        def _():
            gp_copy(1 - side).wait_recv()
        for h in range(HGT):
            put_shifted(gp3, 3 * side, h, gp_halo[side, :, h * WID:(h + 1) * WID].astype(F32))
    phase2(0)
    phase2(1)
    for d in range(2):
        value = conv(0, gp3, d)
        for h in range(HGT):
            gin_f[d, pl.ds(h, CH, stride=HGT), :] = value[:, h * WID:(h + 1) * WID]
        gin_v[:, d] = gin_f[d].reshape(CH, HGT, WID).astype(BF16)
    out_copy = pltpu.make_async_copy(gin_v, gin_hbm.at[0], out_sem)
    out_copy.start()
    phase3(0)
    phase3(1)
    finish(0, g1_ref)
    finish(1, g2_ref)
    out_copy.wait()

    for side, there in ((0, has_prev), (1, has_next)):
        @pl.when(there)
        def _():
            for k in range(3):
                halo_copy(k, side).wait_send()
            gp_copy(side).wait_send()
    for g in range(2):
        pair(g).wait_send()
        all_of(rx1, g, 1, nq - 1).wait_send()
        all_of(rx2, g, 2, nz - 1).wait_send()
        all_of(rx3, g, 3, 2 * nq - 1).wait_send()


def build(mesh, sizes):
    nx, nzh, ny, nzl = sizes
    nq = nx * ny
    nz = nzh * nzl
    per = TILES // (2 * nq)
    total = mesh.shape["dp"] * mesh.shape["space"] * 2 * HGT * WID
    cfg = (nx, nzh, ny, nzl, float(total) ** -0.5)
    any_spec = pl.BlockSpec(memory_space=pl.ANY)
    vmem = pl.BlockSpec(memory_space=pltpu.VMEM)
    dma = pltpu.SemaphoreType.DMA

    def per_device(layer_input, pre_act, cotangent, weight_one, weight_two):
        gin, g1, g2 = pl.pallas_call(
            functools.partial(kernel, cfg),
            out_shape=(
                jax.ShapeDtypeStruct(layer_input.shape, BF16),
                jax.ShapeDtypeStruct((USED, CH, CH), F32),
                jax.ShapeDtypeStruct((USED, CH, CH), F32),
            ),
            in_specs=[any_spec, any_spec, any_spec, vmem, vmem],
            out_specs=(any_spec, vmem, vmem),
            scratch_shapes=[
                pltpu.VMEM((3, CH, 2, HGT, WID), BF16),
                pltpu.VMEM((3, 2, CH, HGT, WID), BF16),
                pltpu.VMEM((3, 4, CH * HGT, WID), F32),
                pltpu.VMEM((384, PLANE), BF16),
                pltpu.VMEM((384, PLANE), BF16),
                pltpu.VMEM((384, PLANE), BF16),
                pltpu.VMEM((384, PLANE), BF16),
                pltpu.VMEM((2, CH, PLANE), F32),
                pltpu.VMEM((2, 96, 288), BF16),
                pltpu.VMEM((2, CH, PLANE), BF16),
                pltpu.VMEM((2, CH * HGT, WID), F32),
                pltpu.VMEM((CH, 2, HGT, WID), BF16),
                pltpu.VMEM((2, TILES, 8, 128), F32),
                pltpu.VMEM((2, TILES // 2, 8, 128), F32),
                pltpu.VMEM((2, nq, per, 8, 128), F32),
                pltpu.VMEM((2, nz, per, 8, 128), F32),
                pltpu.VMEM((2, 2 * nq, per, 8, 128), F32),
                dma((3,)),
                dma,
                dma((3, 2)),
                dma((3, 2)),
                dma((2,)),
                dma((2,)),
                dma((2, 4)),
                dma((2, 4)),
            ],
            compiler_params=pltpu.CompilerParams(
                collective_id=0, has_side_effects=True, vmem_limit_bytes=48 * 1024 * 1024
            ),
        )(layer_input, pre_act, cotangent, weight_one, weight_two)
        shape = weight_one.shape
        return gin, g1.reshape(shape), g2.reshape(shape)

    split = P("dp", None, "space", None, None)
    return jax.shard_map(
        per_device,
        mesh=mesh,
        in_specs=(split, split, split, P(), P()),
        out_specs=(split, P(), P()),
        check_vma=False,
    )


def solution(mesh):
    nzl = 2
    ny = mesh.shape["space"] // nzl
    nx = 4
    nzh = mesh.shape["dp"] // (2 * nx)
    return build(mesh, (nx, nzh, ny, nzl))
```

time: 336 us -> 59.4 us (0.18)
  waiting for transfers between devices: 272 us -> 0 us
  Pallas kernels: 0 us -> 51.6 us
  matrix products: 29.2 us -> 0 us
  between operations: 14.5 us -> 0.65 us
  starting transfers between devices: 10.6 us -> 0 us
    psum x1 -> x0, waiting for transfers between devices: 256 us -> none  [per_device(): gone = lax.psum(gone, ('dp', 'space'))]
    pallas_call x0 -> x1, Pallas kernels: none -> 51.6 us  [per_device(): pl.pallas_call(functools.partial(kernel, cfg), out_shape=(jax.ShapeDtypeS...]
    dot_general x108 -> x0, matrix products: 29.2 us -> none  [the longest x54 15 us: transposed(): jnp.einsum('oi,odhw->idhw', weight[kd, kh, kw], window, preferred_element...]
    ppermute x4 -> x0, waiting for transfers between devices: 16.5 us -> none  [the longest x2 10 us: padded(): lax.ppermute(lax.slice_in_dim(block, 0, width, axis=dim), axis, backward)]
    ppermute x4 -> x0, starting transfers between devices: 10.5 us -> none  [the longest x2 7.93 us: padded(): lax.ppermute(lax.slice_in_dim(block, block.shape[dim] - width, None, axis...]
  transfers between devices with their start and end apart: 5 -> 0, of which waited for: 3 -> 0; matrix products, arithmetic and copies ran while one was open for 1% -> 0% of each run, Pallas kernels for 0% -> 0%
where the time goes in v1:
time: 59.4 us; the launch traced here: 59.2 us
  Pallas kernels  51.6 us (87%)
  local copies, waits for them, and re-layouts  6.94 us (12%)
  between operations  0.65 us (1%)
    pallas_call x1, Pallas kernels, per_device(): pl.pallas_call(functools.partial(kernel, cfg), out_shape=(jax.ShapeDtypeS...  51.6 us
    unnamed x13, local copies, waits for them, and re-layouts  6.94 us

profile of v1, /device:TPU:1, one launch (start us, length us, event | category | flops | bytes accessed | tf_op | source)
XLA Modules:
  0.0 59.2 jit_solution(5634554109792646676)
XLA Ops:
  0.6 0.0 copy-start
  0.6 0.9 %copy-done = bf16[1,32,2,16,128]{4,3,2,1,0:T(8,128)(2,1)S(1)} copy-done((bf16[1,32,2,16,128]{4,3,2,1,0:T(8,128)(2,1)S(1)}, bf16[1,32,2,16,128]{4,3,2,1,0:T(8,128)(2,1)}, u32[]{:S(2)}) %copy-start) | copy-done | bytes 262168
  1.6 0.0 copy-start.1
  1.6 0.9 %copy-done.1 = bf16[1,32,2,16,128]{4,3,2,1,0:T(8,128)(2,1)S(1)} copy-done((bf16[1,32,2,16,128]{4,3,2,1,0:T(8,128)(2,1)S(1)}, bf16[1,32,2,16,128]{4,3,2,1,0:T(8,128)(2,1)}, u32[]{:S(2)}) %copy-start.1) | copy-done | bytes 262168
  2.5 0.0 copy-start.2
  2.5 0.9 %copy-done.2 = bf16[1,32,2,16,128]{4,3,2,1,0:T(8,128)(2,1)S(1)} copy-done((bf16[1,32,2,16,128]{4,3,2,1,0:T(8,128)(2,1)S(1)}, bf16[1,32,2,16,128]{4,3,2,1,0:T(8,128)(2,1)}, u32[]{:S(2)}) %copy-start.2) | copy-done | bytes 262168
  3.5 0.0 copy-start.3
  3.5 0.9 %copy-done.3 = bf16[3,3,3,32,32]{4,3,2,1,0:T(8,128)(2,1)S(1)} copy-done((bf16[3,3,3,32,32]{4,3,2,1,0:T(8,128)(2,1)S(1)}, bf16[3,3,3,32,32]{4,3,2,1,0:T(8,128)(2,1)}, u32[]{:S(2)}) %copy-start.3) | copy-done | bytes 55320
  4.4 0.0 copy-start.4
  4.4 0.9 %copy-done.4 = bf16[3,3,3,32,32]{4,3,2,1,0:T(8,128)(2,1)S(1)} copy-done((bf16[3,3,3,32,32]{4,3,2,1,0:T(8,128)(2,1)S(1)}, bf16[3,3,3,32,32]{4,3,2,1,0:T(8,128)(2,1)}, u32[]{:S(2)}) %copy-start.4) | copy-done | bytes 55320
  5.4 51.6 %shard_map.76 = (bf16[1,32,2,16,128]{4,3,2,1,0:T(8,128)(2,1)S(1)}, f32[27,32,32]{2,1,0:T(8,128)S(1)}, f32[27,32,32]{2,1,0:T(8,128)S(1)}) custom-call(bf16[1,32,2,16,128]{4,3,2,1,0:T(8,128)(2,1)S(1)} %copy-done, bf16[1,32,2,16,128]{4,3,2,1,0:T(8,128)(2,1)S(1)} %copy-done.1, bf16[1,32,2,16,128]{4,3,2,1,0:T(8,128)(2,1)S(1)} %copy-done.2, ...), custom_call_target="tpu_custom_call" | custom-call | tf_op jit(solution)/shard_map/pallas_call | solution.py:349
  57.0 0.7 %copy.11 = bf16[1,32,2,16,128]{4,3,2,1,0:T(8,128)(2,1)} copy(bf16[1,32,2,16,128]{4,3,2,1,0:T(8,128)(2,1)S(1)} %get-tuple-element.12) | data formatting | bytes 524288
  57.7 0.8 %copy.12 = f32[3,3,3,32,32]{4,3,2,1,0:T(8,128)} copy(f32[3,3,3,32,32]{4,3,2,1,0:T(8,128)S(1)} %bitcast.3) | data formatting | bytes 221184
  58.5 0.8 %copy.13 = f32[3,3,3,32,32]{4,3,2,1,0:T(8,128)} copy(f32[3,3,3,32,32]{4,3,2,1,0:T(8,128)S(1)} %bitcast.2) | data formatting | bytes 221184
Async XLA Ops:
  0.6 1.0 %copy-start = (bf16[1,32,2,16,128]{4,3,2,1,0:T(8,128)(2,1)S(1)}, bf16[1,32,2,16,128]{4,3,2,1,0:T(8,128)(2,1)}, u32[]{:S(2)}) copy-start(bf16[1,32,2,16,128]{4,3,2,1,0:T(8,128)(2,1)} %src_hbm.1) | copy-start | bytes 786436
  1.6 0.9 %copy-start.1 = (bf16[1,32,2,16,128]{4,3,2,1,0:T(8,128)(2,1)S(1)}, bf16[1,32,2,16,128]{4,3,2,1,0:T(8,128)(2,1)}, u32[]{:S(2)}) copy-start(bf16[1,32,2,16,128]{4,3,2,1,0:T(8,128)(2,1)} %pre_hbm.1) | copy-start | bytes 786436
  2.5 0.9 %copy-start.2 = (bf16[1,32,2,16,128]{4,3,2,1,0:T(8,128)(2,1)S(1)}, bf16[1,32,2,16,128]{4,3,2,1,0:T(8,128)(2,1)}, u32[]{:S(2)}) copy-start(bf16[1,32,2,16,128]{4,3,2,1,0:T(8,128)(2,1)} %cot_hbm.1) | copy-start | bytes 786436
  3.5 0.9 %copy-start.3 = (bf16[3,3,3,32,32]{4,3,2,1,0:T(8,128)(2,1)S(1)}, bf16[3,3,3,32,32]{4,3,2,1,0:T(8,128)(2,1)}, u32[]{:S(2)}) copy-start(bf16[3,3,3,32,32]{4,3,2,1,0:T(8,128)(2,1)} %w1_ref.1) | copy-start | bytes 165892
  4.4 0.9 %copy-start.4 = (bf16[3,3,3,32,32]{4,3,2,1,0:T(8,128)(2,1)S(1)}, bf16[3,3,3,32,32]{4,3,2,1,0:T(8,128)(2,1)}, u32[]{:S(2)}) copy-start(bf16[3,3,3,32,32]{4,3,2,1,0:T(8,128)(2,1)} %w2_ref.1) | copy-start | bytes 165892

commit v2 on v1

--- a/solution.py
+++ b/solution.py
@@ -23,11 +23,11 @@
 
 def kernel(
     cfg,
-    src_hbm, pre_hbm, cot_hbm, w1_ref, w2_ref,
-    gin_hbm, g1_ref, g2_ref,
-    own, halo, rows_scr, cot3, act3, src3, gp3, preT, wcat, gp_halo, gin_f, gin_v,
+    src_hbm, pre_hbm, cot_hbm, w1_hbm, w2_hbm,
+    gin_ref, g1_ref, g2_ref,
+    own, weights, halo, rows_scr, cot3, act3, src3, gp3, preT, wcat, gp_halo, gin_f, gacc,
     parts, rx0, rx1, rx2, rx3,
-    load_sem, out_sem, hs, hr, gs, gr, send_sem, recv_sem,
+    load_sem, known_x, known_y, known_z, known_c, hs, hr, gs, gr, send_sem, recv_sem,
 ):
     nx, nzh, ny, nzl, scale = cfg
     nq = nx * ny
@@ -57,6 +57,17 @@
     has_prev = sp > 0
     has_next = sp < nsp - 1
     barrier = pltpu.get_barrier_semaphore()
+    partner = (dp + 1 - 2 * core, sp)
+
+    def at_x(r):
+        return ((r * nzh + zh) * 2 + core, sp)
+
+    def at_y(r):
+        return (dp, r * nzl + zl)
+
+    beside_x = (at_x(lax.rem(x + 1, nx)), at_x(lax.rem(x + nx - 1, nx)))
+    beside_y = (at_y(lax.rem(y + 1, ny)), at_y(lax.rem(y + ny - 1, ny)))
+    beside_z = (z_peer(lax.rem(z + 1, nz)), z_peer(lax.rem(z + nz - 1, nz)))
 
     @pl.when(has_prev)
     def _():
@@ -66,24 +77,18 @@
     def _():
         pl.semaphore_signal(barrier, inc=1, device_id=(dp, sp + 1))
 
-    def greet_plane(k, carry):
-        pl.semaphore_signal(barrier, inc=1, device_id=plane_peer(lax.rem(me + k, 2 * nq)))
-        return carry
-
-    def greet_z(k, carry):
-        pl.semaphore_signal(barrier, inc=1, device_id=z_peer(lax.rem(z + k, nz)))
-        return carry
-
-    lax.fori_loop(1, 2 * nq, greet_plane, 0)
-    lax.fori_loop(1, nz, greet_z, 0)
+    for device in beside_x + beside_y + beside_z + (partner,):
+        pl.semaphore_signal(barrier, inc=1, device_id=device)
 
     args = (cot_hbm, src_hbm, pre_hbm)
-    loads = [pltpu.make_async_copy(args[k].at[0], own.at[k], load_sem.at[k]) for k in range(3)]
-    for copy in loads:
+    loads = [pltpu.make_async_copy(args[k].at[0], own.at[k], load_sem.at[k]) for k in (0, 1, 2)]
+    weight_loads = [
+        pltpu.make_async_copy((w1_hbm, w2_hbm)[g], weights.at[g], load_sem.at[3 + g]) for g in range(2)
+    ]
+    for copy in (loads[0], weight_loads[1], loads[2], loads[1], weight_loads[0]):
         copy.start()
 
-    expected = 2 * nq - 1 + nz - 1 + has_prev.astype(jnp.int32) + has_next.astype(jnp.int32)
-    pl.semaphore_wait(barrier, expected)
+    pl.semaphore_wait(barrier, 7 + has_prev.astype(jnp.int32) + has_next.astype(jnp.int32))
 
     def halo_copy(k, side):
         return pltpu.make_async_remote_copy(
@@ -94,21 +99,36 @@
             device_id=(dp, sp - 1 if side == 0 else sp + 1),
         )
 
-    for side, there in ((0, has_prev), (1, has_next)):
-        @pl.when(there)
-        def _():
-            for k in range(3):
+    sides = ((0, has_prev), (1, has_next))
+    for k in range(2):
+        for side, there in sides:
+            @pl.when(there)
+            def _():
                 halo_copy(k, side).start()
 
+    for side, there in sides:
         @pl.when(jnp.logical_not(there))
         def _():
-            halo[:, side] = jnp.zeros((3, CH, HGT, WID), BF16)
-
-    for g, w_ref in ((0, w1_ref), (1, w2_ref)):
+            halo[:, side] = jnp.zeros((2, CH, HGT, WID), BF16)
+
+    def tell(sem, step, devices):
+        for device in devices:
+            pl.semaphore_signal(sem.at[step], inc=1, device_id=device)
+
+    def learn(sem, step, count=2):
+        pl.semaphore_wait(sem.at[step], count)
+
+    tell(known_x, 0, beside_x)
+    tell(known_z, 0, beside_z)
+
+    def spread(g):
+        weight_loads[g].wait()
         for a in range(3):
             for b in range(3):
-                block = w_ref[a, b].reshape(3 * CH, CH).astype(F32)
+                block = weights[g, a, b].reshape(3 * CH, CH).astype(F32)
                 wcat[g, b * CH:(b + 1) * CH, (2 - a) * 96:(3 - a) * 96] = block.T.astype(BF16)
+
+    spread(1)
 
     lane = lax.broadcasted_iota(jnp.int32, (CH, WID), 1)
 
@@ -144,24 +164,8 @@
             elif k == 1:
                 put_rows(src3, p, h, value)
             else:
-                put_rows(act3, p, h, leaky(value))
-                if 1 <= p <= 2:
-                    preT[p - 1, :, h * WID:(h + 1) * WID] = value
-
-    for p in range(4):
-        clear_edges(src3, p)
-        clear_edges(act3, p)
-    for k in range(3):
-        loads[k].wait()
-        for d in range(2):
-            take(k, d + 1, own[k, :, d])
-
-    for k in range(3):
-        for side, there in ((0, has_prev), (1, has_next)):
-            @pl.when(there)
-            def _():
-                halo_copy(k, 1 - side).wait_recv()
-            take(k, 3 * side, halo[k, side])
+                put_rows(act3, p - 1, h, leaky(value))
+                preT[p - 1, :, h * WID:(h + 1) * WID] = value
 
     def conv(g, ref, d):
         y3 = jnp.dot(wcat[g], ref[d * 96:(d + 3) * 96, :], preferred_element_type=F32)
@@ -181,6 +185,9 @@
             )
             total = term if total is None else total + term
         return total
+
+    def partial(low, top):
+        return lax.dot_general(low, top, (((1,), (1,)), ((), ())), preferred_element_type=F32)
 
     lane8 = lax.broadcasted_iota(jnp.int32, (9, 8, 128), 2) // CH
 
@@ -206,7 +213,7 @@
 
     def pair(g):
         other = 1 - core
-        return rdma(parts.at[g, pl.ds(other * half, half)], rx0.at[g], g, 0, (dp + other - core, sp))
+        return rdma(parts.at[g, pl.ds(other * half, half)], rx0.at[g], g, 0, partner)
 
     def phase1(g):
         pair(g).wait_recv()
@@ -221,7 +228,7 @@
         lax.fori_loop(1, nq, send, 0)
 
     def all_of(ref, g, phase, count):
-        return rdma(ref.at[g, pl.ds(0, count)], ref.at[g, pl.ds(0, count)], g, phase, (dp + 1 - 2 * core, sp))
+        return rdma(ref.at[g, pl.ds(0, count)], ref.at[g, pl.ds(0, count)], g, phase, partner)
 
     def phase2(g):
         all_of(rx1, g, 1, nq - 1).wait_recv()
@@ -268,11 +275,6 @@
             piece = tiles if j == 0 else pltpu.roll(tiles, 128 - CH * j, 2)
             out_ref[:, 8 * j:8 * (j + 1), :] = piece[:, :, :CH]
 
-    for d in range(2):
-        value = conv(1, cot3, d) * jnp.where(preT[d] > 0, 1.0, 0.3)
-        for h in range(HGT):
-            put_shifted(gp3, d + 1, h, value[:, h * WID:(h + 1) * WID].astype(BF16).astype(F32))
-
     def gp_copy(side):
         return pltpu.make_async_remote_copy(
             src_ref=gp3.at[pl.ds((1 + side) * 96 + CH, CH)],
@@ -282,49 +284,90 @@
             device_id=(dp, sp - 1 if side == 0 else sp + 1),
         )
 
-    for side, there in ((0, has_prev), (1, has_next)):
+    loads[0].wait()
+    for d in range(2):
+        take(0, d + 1, own[0, :, d])
+    learn(known_x, 0)
+    learn(known_z, 0)
+    tell(known_y, 0, beside_y)
+    tell(known_z, 1, beside_z)
+    for p in range(2):
+        clear_edges(act3, p)
+    loads[2].wait()
+    for d in range(2):
+        take(2, d + 1, own[2, :, d])
+    learn(known_y, 0)
+    learn(known_z, 1)
+    tell(known_y, 1, beside_y)
+    tell(known_z, 2, beside_z)
+    for p in range(4):
+        clear_edges(src3, p)
+    loads[1].wait()
+    for d in range(2):
+        take(1, d + 1, own[1, :, d])
+    learn(known_y, 1)
+    learn(known_z, 2)
+    tell(known_c, 0, (partner,))
+    here = partial(act3[...], cot3[96:224, :])
+    gacc[96:288] = here
+    here = partial(act3[...], cot3[192:320, :])
+    gacc[0:96] = here[:96]
+    gacc[96:192] += here[96:]
+    spread(0)
+
+    for side, there in sides:
         @pl.when(there)
         def _():
+            halo_copy(0, 1 - side).wait_recv()
+        take(0, 3 * side, halo[0, side])
+        value = conv(1, cot3, side) * jnp.where(preT[side] > 0, 1.0, 0.3)
+        for h in range(HGT):
+            put_shifted(gp3, side + 1, h, value[:, h * WID:(h + 1) * WID].astype(BF16).astype(F32))
+
+        @pl.when(there)
+        def _():
             gp_copy(side).start()
 
         @pl.when(jnp.logical_not(there))
         def _():
             gp_halo[side] = jnp.zeros((CH, PLANE), BF16)
 
-    gp3[0:96, :] = jnp.zeros((96, PLANE), BF16)
-    gp3[288:384, :] = jnp.zeros((96, PLANE), BF16)
+    for side, there in sides:
+        @pl.when(there)
+        def _():
+            halo_copy(1, 1 - side).wait_recv()
+        take(1, 3 * side, halo[1, side])
     pack(0, kernel_grad(src3, gp3))
     pair(0).start()
-    pack(1, kernel_grad(act3, cot3))
+    gacc[192:288] += partial(act3[0:96, :], cot3[0:128, :])
+    gacc[0:96] += partial(act3[96:192, :], cot3[288:416, :])
+    pack(1, gacc[...])
     pair(1).start()
     phase1(0)
     phase1(1)
-
-    for side, there in ((0, has_prev), (1, has_next)):
+    learn(known_c, 0, 1)
+    phase2(0)
+    phase2(1)
+    for side, there in sides:
         @pl.when(there)
         def _():
             gp_copy(1 - side).wait_recv()
         for h in range(HGT):
             put_shifted(gp3, 3 * side, h, gp_halo[side, :, h * WID:(h + 1) * WID].astype(F32))
-    phase2(0)
-    phase2(1)
     for d in range(2):
         value = conv(0, gp3, d)
         for h in range(HGT):
             gin_f[d, pl.ds(h, CH, stride=HGT), :] = value[:, h * WID:(h + 1) * WID]
-        gin_v[:, d] = gin_f[d].reshape(CH, HGT, WID).astype(BF16)
-    out_copy = pltpu.make_async_copy(gin_v, gin_hbm.at[0], out_sem)
-    out_copy.start()
+        gin_ref[0, :, d] = gin_f[d].reshape(CH, HGT, WID).astype(BF16)
     phase3(0)
     phase3(1)
     finish(0, g1_ref)
     finish(1, g2_ref)
-    out_copy.wait()
-
-    for side, there in ((0, has_prev), (1, has_next)):
+
+    for side, there in sides:
         @pl.when(there)
         def _():
-            for k in range(3):
+            for k in range(2):
                 halo_copy(k, side).wait_send()
             gp_copy(side).wait_send()
     for g in range(2):
@@ -334,6 +377,15 @@
         all_of(rx3, g, 3, 2 * nq - 1).wait_send()
 
 
+def write_out(gin_ref, g1_ref, g2_ref, gin_hbm, g1_hbm, g2_hbm, sem):
+    pairs = ((gin_ref, gin_hbm), (g1_ref, g1_hbm), (g2_ref, g2_hbm))
+    copies = [pltpu.make_async_copy(here, there, sem.at[k]) for k, (here, there) in enumerate(pairs)]
+    for copy in copies:
+        copy.start()
+    for copy in copies:
+        copy.wait()
+
+
 def build(mesh, sizes):
     nx, nzh, ny, nzl = sizes
     nq = nx * ny
@@ -341,11 +393,15 @@
     per = TILES // (2 * nq)
     total = mesh.shape["dp"] * mesh.shape["space"] * 2 * HGT * WID
     cfg = (nx, nzh, ny, nzl, float(total) ** -0.5)
-    any_spec = pl.BlockSpec(memory_space=pl.ANY)
+    hbm = pl.BlockSpec(memory_space=pltpu.HBM)
     vmem = pl.BlockSpec(memory_space=pltpu.VMEM)
     dma = pltpu.SemaphoreType.DMA
 
     def per_device(layer_input, pre_act, cotangent, weight_one, weight_two):
+        held = [
+            pltpu.with_memory_space_constraint(v, pltpu.HBM)
+            for v in (layer_input, pre_act, cotangent, weight_one, weight_two)
+        ]
         gin, g1, g2 = pl.pallas_call(
             functools.partial(kernel, cfg),
             out_shape=(
@@ -353,30 +409,34 @@
                 jax.ShapeDtypeStruct((USED, CH, CH), F32),
                 jax.ShapeDtypeStruct((USED, CH, CH), F32),
             ),
-            in_specs=[any_spec, any_spec, any_spec, vmem, vmem],
-            out_specs=(any_spec, vmem, vmem),
+            in_specs=[hbm] * 5,
+            out_specs=(vmem, vmem, vmem),
             scratch_shapes=[
                 pltpu.VMEM((3, CH, 2, HGT, WID), BF16),
-                pltpu.VMEM((3, 2, CH, HGT, WID), BF16),
+                pltpu.VMEM((2, 3, 3, 3, CH, CH), BF16),
+                pltpu.VMEM((2, 2, CH, HGT, WID), BF16),
                 pltpu.VMEM((3, 4, CH * HGT, WID), F32),
-                pltpu.VMEM((384, PLANE), BF16),
-                pltpu.VMEM((384, PLANE), BF16),
+                pltpu.VMEM((416, PLANE), BF16),
+                pltpu.VMEM((192, PLANE), BF16),
                 pltpu.VMEM((384, PLANE), BF16),
                 pltpu.VMEM((384, PLANE), BF16),
                 pltpu.VMEM((2, CH, PLANE), F32),
                 pltpu.VMEM((2, 96, 288), BF16),
                 pltpu.VMEM((2, CH, PLANE), BF16),
                 pltpu.VMEM((2, CH * HGT, WID), F32),
-                pltpu.VMEM((CH, 2, HGT, WID), BF16),
+                pltpu.VMEM((288, 128), F32),
                 pltpu.VMEM((2, TILES, 8, 128), F32),
                 pltpu.VMEM((2, TILES // 2, 8, 128), F32),
                 pltpu.VMEM((2, nq, per, 8, 128), F32),
                 pltpu.VMEM((2, nz, per, 8, 128), F32),
                 pltpu.VMEM((2, 2 * nq, per, 8, 128), F32),
-                dma((3,)),
-                dma,
-                dma((3, 2)),
-                dma((3, 2)),
+                dma((5,)),
+                pltpu.SemaphoreType.REGULAR((1,)),
+                pltpu.SemaphoreType.REGULAR((2,)),
+                pltpu.SemaphoreType.REGULAR((3,)),
+                pltpu.SemaphoreType.REGULAR((1,)),
+                dma((2, 2)),
+                dma((2, 2)),
                 dma((2,)),
                 dma((2,)),
                 dma((2, 4)),
@@ -385,7 +445,15 @@
             compiler_params=pltpu.CompilerParams(
                 collective_id=0, has_side_effects=True, vmem_limit_bytes=48 * 1024 * 1024
             ),
-        )(layer_input, pre_act, cotangent, weight_one, weight_two)
+        )(*held)
+        gin, g1, g2 = pl.pallas_call(
+            write_out,
+            out_shape=tuple(jax.ShapeDtypeStruct(v.shape, v.dtype) for v in (gin, g1, g2)),
+            in_specs=[vmem] * 3,
+            out_specs=(hbm,) * 3,
+            scratch_shapes=[dma((3,))],
+            compiler_params=pltpu.CompilerParams(vmem_limit_bytes=8 * 1024 * 1024),
+        )(gin, g1, g2)
         shape = weight_one.shape
         return gin, g1.reshape(shape), g2.reshape(shape)
 

time: 59.4 us -> 43.8 us (0.74)
  Pallas kernels: 51.6 us -> 43 us
  local copies, waits for them, and re-layouts: 6.94 us -> 0 us
    pallas_call x1, Pallas kernels: 51.6 us -> 42 us  [per_device(): pl.pallas_call(functools.partial(kernel, cfg), out_shape=(jax.ShapeDtypeS...]
    unnamed x13 -> x0, local copies, waits for them, and re-layouts: 6.94 us -> none
    pallas_call x0 -> x1, Pallas kernels: none -> 1.02 us  [per_device(): pl.pallas_call(write_out, out_shape=tuple((jax.ShapeDtypeStruct(v.shape,...]
where the time goes in v2:
time: 43.8 us; the launch traced here: 43.7 us
  Pallas kernels  43 us (98%)
  between operations  0.64 us (1%)
    pallas_call x1, Pallas kernels, per_device(): pl.pallas_call(functools.partial(kernel, cfg), out_shape=(jax.ShapeDtypeS...  42 us
    pallas_call x1, Pallas kernels, per_device(): pl.pallas_call(write_out, out_shape=tuple((jax.ShapeDtypeStruct(v.shape,...  1.02 us

profile of v2, /device:TPU:1, one launch (start us, length us, event | category | flops | bytes accessed | tf_op | source)
XLA Modules:
  0.0 43.7 jit_solution(4891994806964191984)
XLA Ops:
  0.6 42.0 %shard_map.76 = (bf16[1,32,2,16,128]{4,3,2,1,0:T(8,128)(2,1)S(1)}, f32[27,32,32]{2,1,0:T(8,128)S(1)}, f32[27,32,32]{2,1,0:T(8,128)S(1)}) custom-call(bf16[1,32,2,16,128]{4,3,2,1,0:T(8,128)(2,1)} %src_hbm.1, bf16[1,32,2,16,128]{4,3,2,1,0:T(8,128)(2,1)} %pre_hbm.1, bf16[1,32,2,16,128]{4,3,2,1,0:T(8,128)(2,1)} %cot_hbm.1, bf16[3,3,3,32,32]{4,3,2,1,0:T(8,128)(2,1)} %w1_hbm.1, ...), custom_call_target="tpu_custom_call" | custom-call | tf_op jit(solution)/shard_map/pallas_call | solution.py:405
  42.7 1.0 %shard_map.77 = (bf16[1,32,2,16,128]{4,3,2,1,0:T(8,128)(2,1)}, f32[27,32,32]{2,1,0:T(8,128)}, f32[27,32,32]{2,1,0:T(8,128)}) custom-call(bf16[1,32,2,16,128]{4,3,2,1,0:T(8,128)(2,1)S(1)} %get-tuple-element.9.gin_ref, f32[27,32,32]{2,1,0:T(8,128)S(1)} %get-tuple-element.10.g1_ref, f32[27,32,32]{2,1,0:T(8,128)S(1)} %get-tuple-element.11.g2_ref), custom_call_target="tpu_custom_call" | custom-call | tf_op jit(solution)/shard_map/pallas_call | solution.py:449

commit v3 on v2

--- a/solution.py
+++ b/solution.py
@@ -173,18 +173,6 @@
         first = jnp.concatenate([y3[0:CH, WID:], blank], axis=1)
         last = jnp.concatenate([blank, y3[2 * CH:, :PLANE - WID]], axis=1)
         return y3[CH:2 * CH] + first + last
-
-    def kernel_grad(low, top):
-        total = None
-        for d in range(2):
-            term = lax.dot_general(
-                low[d * 96:(d + 3) * 96, :],
-                top[(d + 1) * 96:(d + 1) * 96 + 128, :],
-                (((1,), (1,)), ((), ())),
-                preferred_element_type=F32,
-            )
-            total = term if total is None else total + term
-        return total
 
     def partial(low, top):
         return lax.dot_general(low, top, (((1,), (1,)), ((), ())), preferred_element_type=F32)
@@ -309,10 +297,10 @@
     learn(known_z, 2)
     tell(known_c, 0, (partner,))
     here = partial(act3[...], cot3[96:224, :])
-    gacc[96:288] = here
+    gacc[1, 96:288] = here
     here = partial(act3[...], cot3[192:320, :])
-    gacc[0:96] = here[:96]
-    gacc[96:192] += here[96:]
+    gacc[1, 0:96] = here[:96]
+    gacc[1, 96:192] += here[96:]
     spread(0)
 
     for side, there in sides:
@@ -324,6 +312,7 @@
         for h in range(HGT):
             put_shifted(gp3, side + 1, h, value[:, h * WID:(h + 1) * WID].astype(BF16).astype(F32))
 
+    for side, there in sides:
         @pl.when(there)
         def _():
             gp_copy(side).start()
@@ -331,23 +320,33 @@
         @pl.when(jnp.logical_not(there))
         def _():
             gp_halo[side] = jnp.zeros((CH, PLANE), BF16)
+
+    gacc[1, 192:288] += partial(act3[0:96, :], cot3[0:128, :])
+    gacc[1, 0:96] += partial(act3[96:192, :], cot3[288:416, :])
+    pack(1, gacc[1])
+    pair(1).start()
+    here = partial(src3[96:288, :], gp3[96:224, :])
+    gacc[0, 96:288] = here
+    here = partial(src3[96:288, :], gp3[192:320, :])
+    gacc[0, 0:96] = here[:96]
+    gacc[0, 96:192] += here[96:]
+    phase1(1)
 
     for side, there in sides:
         @pl.when(there)
         def _():
             halo_copy(1, 1 - side).wait_recv()
         take(1, 3 * side, halo[1, side])
-    pack(0, kernel_grad(src3, gp3))
+        gacc[0, 192 * side:192 * side + 96] += partial(
+            src3[288 * side:288 * side + 96, :], gp3[96 * side + 96:96 * side + 224, :]
+        )
+    pack(0, gacc[0])
     pair(0).start()
-    gacc[192:288] += partial(act3[0:96, :], cot3[0:128, :])
-    gacc[0:96] += partial(act3[96:192, :], cot3[288:416, :])
-    pack(1, gacc[...])
-    pair(1).start()
     phase1(0)
-    phase1(1)
+    phase2(1)
+    phase2(0)
     learn(known_c, 0, 1)
-    phase2(0)
-    phase2(1)
+    phase3(1)
     for side, there in sides:
         @pl.when(there)
         def _():
@@ -360,9 +359,8 @@
             gin_f[d, pl.ds(h, CH, stride=HGT), :] = value[:, h * WID:(h + 1) * WID]
         gin_ref[0, :, d] = gin_f[d].reshape(CH, HGT, WID).astype(BF16)
     phase3(0)
-    phase3(1)
+    finish(1, g2_ref)
     finish(0, g1_ref)
-    finish(1, g2_ref)
 
     for side, there in sides:
         @pl.when(there)
@@ -424,7 +422,7 @@
                 pltpu.VMEM((2, 96, 288), BF16),
                 pltpu.VMEM((2, CH, PLANE), BF16),
                 pltpu.VMEM((2, CH * HGT, WID), F32),
-                pltpu.VMEM((288, 128), F32),
+                pltpu.VMEM((2, 288, 128), F32),
                 pltpu.VMEM((2, TILES, 8, 128), F32),
                 pltpu.VMEM((2, TILES // 2, 8, 128), F32),
                 pltpu.VMEM((2, nq, per, 8, 128), F32),

time: 43.8 us -> 41.8 us (0.954)
  Pallas kernels: 43 us -> 41.1 us
    pallas_call x1, Pallas kernels: 42 us -> 40.1 us  [per_device(): pl.pallas_call(functools.partial(kernel, cfg), out_shape=(jax.ShapeDtypeS...]
where the time goes in v3:
time: 41.8 us; the launch traced here: 41.7 us
  Pallas kernels  41.1 us (98%)
  between operations  0.64 us (2%)
    pallas_call x1, Pallas kernels, per_device(): pl.pallas_call(functools.partial(kernel, cfg), out_shape=(jax.ShapeDtypeS...  40.1 us
    pallas_call x1, Pallas kernels, per_device(): pl.pallas_call(write_out, out_shape=tuple((jax.ShapeDtypeStruct(v.shape,...  1.02 us

profile of v3, /device:TPU:1, one launch (start us, length us, event | category | flops | bytes accessed | tf_op | source)
XLA Modules:
  0.0 41.7 jit_solution(9783056074561835002)
XLA Ops:
  0.6 40.1 %shard_map.76 = (bf16[1,32,2,16,128]{4,3,2,1,0:T(8,128)(2,1)S(1)}, f32[27,32,32]{2,1,0:T(8,128)S(1)}, f32[27,32,32]{2,1,0:T(8,128)S(1)}) custom-call(bf16[1,32,2,16,128]{4,3,2,1,0:T(8,128)(2,1)} %src_hbm.1, bf16[1,32,2,16,128]{4,3,2,1,0:T(8,128)(2,1)} %pre_hbm.1, bf16[1,32,2,16,128]{4,3,2,1,0:T(8,128)(2,1)} %cot_hbm.1, bf16[3,3,3,32,32]{4,3,2,1,0:T(8,128)(2,1)} %w1_hbm.1, ...), custom_call_target="tpu_custom_call" | custom-call | tf_op jit(solution)/shard_map/pallas_call | solution.py:403
  40.7 1.0 %shard_map.77 = (bf16[1,32,2,16,128]{4,3,2,1,0:T(8,128)(2,1)}, f32[27,32,32]{2,1,0:T(8,128)}, f32[27,32,32]{2,1,0:T(8,128)}) custom-call(bf16[1,32,2,16,128]{4,3,2,1,0:T(8,128)(2,1)S(1)} %get-tuple-element.9.gin_ref, f32[27,32,32]{2,1,0:T(8,128)S(1)} %get-tuple-element.10.g1_ref, f32[27,32,32]{2,1,0:T(8,128)S(1)} %get-tuple-element.11.g2_ref), custom_call_target="tpu_custom_call" | custom-call | tf_op jit(solution)/shard_map/pallas_call | solution.py:447
